TPU v7x, 32 devices: a whole 2x2x4 slice. The times are simulated.
32 devices in a mesh: dp: 2 (over core), row: 4 (over y, x), col: 4 (over z).
Axes of the slice: x: 2, y: 2, z: 4, core: 2. Of those that a mesh axis runs over, the one named last changes fastest.
Arguments:
- tokens: bfloat16 [256, 8192], P(('dp', 'col'), 'row'), may hold values from -6 to 6
- cotangent: bfloat16 [256, 8192], P(('dp', 'col'), 'row'), may hold values from -6 to 6
- weight: bfloat16 [8192, 16384], P('row', 'col'), may hold values from -0.125 to 0.125
- block_mask: int32 [32, 64], P('row', 'col'), may hold values 0 or 1
Outputs:
- output: bfloat16 [256, 8192], P(('dp', 'col'), 'row')
- input_grad: bfloat16 [256, 8192], P(('dp', 'col'), 'row')
- weight_grad: float32 [8192, 2, 8192], P('row', 'dp', 'col')
Inputs may be any that keep to these rules, and one draw needn't show every extreme that they name: block_mask holds only 0 and 1.
All inputs are finite; a program needn't handle non-finite values. No bound on the sum of `block_mask` on one device may be relied on, other than what follows from the above.
Results may differ from a plain program's by a relative error of at most 0.0032.
Values may be sent and summed in bfloat16 or wider, within the bound.
A program may use at most 128 MiB of HBM per device.

v0:
```python
import math
import jax
import jax.numpy as jnp
from jax import lax
from jax.sharding import PartitionSpec as P

BLOCK = 256


def partner(block, axis, stride):
    count = lax.axis_size(axis)
    route = []
    for low in range(count):
        high = low | 1 << stride
        if high != low and high < count:
            route += [(low, high), (high, low)]
    return lax.ppermute(block, axis, route)


def expand_mask(block_mask):
    kept_blocks = block_mask.astype(jnp.bfloat16)
    return jnp.repeat(jnp.repeat(kept_blocks, BLOCK, axis=0), BLOCK, axis=1)


def slope_times(grad_hidden, pre):
    sigmoid_pre = jax.nn.sigmoid(pre)
    return (grad_hidden * sigmoid_pre * (1.0 + pre * (1.0 - sigmoid_pre))).astype(jnp.bfloat16)


def times_transpose(left, masked):
    return lax.dot_general(
        left, masked, (((1,), (1,)), ((), ())), preferred_element_type=jnp.float32
    )


def on_device(tokens, cotangent, weight, block_mask):
    kept = expand_mask(block_mask)
    masked = weight * kept
    tok_count = tokens.shape[0]
    tok_rows, cot_rows = (
        lax.all_gather(tokens, "col", axis=0, tiled=True),
        lax.all_gather(cotangent, "col", axis=0, tiled=True),
    )
    pre_part = jnp.dot(tok_rows, masked, preferred_element_type=jnp.float32)
    pre = lax.psum(pre_part, "row")
    hidden = jax.nn.silu(pre).astype(jnp.bfloat16)
    grad_part = jnp.dot(cot_rows, masked, preferred_element_type=jnp.float32)
    grad_hidden = lax.psum(grad_part, "row")
    grad_pre = slope_times(grad_hidden, pre)
    projected = lax.psum_scatter(
        times_transpose(hidden, masked), "col", scatter_dimension=0, tiled=True
    )
    output = (tokens.astype(jnp.float32) + projected).astype(jnp.bfloat16)
    back = lax.psum_scatter(
        times_transpose(grad_pre, masked), "col", scatter_dimension=0, tiled=True
    )
    input_grad = (cotangent.astype(jnp.float32) + back).astype(jnp.bfloat16)
    tok_total = tok_count * lax.axis_size("col") * lax.axis_size("dp")
    norm_scale = 1.0 / math.sqrt(tok_total)
    feat_rows = masked.shape[0]
    share_cols = masked.shape[1] // lax.axis_size("dp")
    dp_index = lax.axis_index("dp")
    low_bit = dp_index % 2
    groups = lax.axis_size("dp") // 2
    row_total = hidden.shape[0]
    hid_split = hidden.reshape(row_total, groups, 2, share_cols)
    grad_split = grad_pre.reshape(row_total, groups, 2, share_cols)
    hid_class = lax.dynamic_index_in_dim(hid_split, low_bit, 2, keepdims=False)
    grad_class = lax.dynamic_index_in_dim(grad_split, low_bit, 2, keepdims=False)
    hid_other = lax.dynamic_index_in_dim(hid_split, 1 - low_bit, 2, keepdims=False)
    grad_other = lax.dynamic_index_in_dim(grad_split, 1 - low_bit, 2, keepdims=False)
    other_tok, other_cot, other_hid, other_grad = partner(
        (tok_rows, cot_rows, hid_other, grad_other), "dp", 0
    )
    pair_tok = jnp.concatenate([tok_rows, other_tok], axis=0)
    pair_cot = jnp.concatenate([cot_rows, other_cot], axis=0)
    pair_hid = jnp.concatenate([hid_class, other_hid], axis=0)
    pair_grad = jnp.concatenate([grad_class, other_grad], axis=0)
    partial_value = jnp.einsum(
        "td,tqj->qdj", pair_cot, pair_hid, preferred_element_type=jnp.float32
    )
    partial_value = partial_value + jnp.einsum(
        "td,tqj->qdj", pair_tok, pair_grad, preferred_element_type=jnp.float32
    )
    bit_count = lax.axis_size("dp").bit_length() - 1
    for bit_level in range(bit_count - 1, 0, -1):
        halves = partial_value.reshape(2, partial_value.shape[0] // 2, feat_rows, share_cols)
        my_half = dp_index // 2**bit_level % 2
        keep_part = lax.dynamic_index_in_dim(halves, my_half, 0, keepdims=False)
        send_part = lax.dynamic_index_in_dim(halves, 1 - my_half, 0, keepdims=False)
        partial_value = keep_part + partner(send_part, "dp", bit_level)
    kept_share = lax.dynamic_slice_in_dim(kept, dp_index * share_cols, share_cols, 1)
    summed = partial_value[0] * kept_share.astype(jnp.float32) * norm_scale
    weight_grad = summed.reshape(feat_rows, 1, share_cols)
    return (output, input_grad, weight_grad)


def solution(mesh):
    in_specs = (P(("dp", "col"), "row"), P(("dp", "col"), "row"), P("row", "col"), P("row", "col"))
    out_specs = (P(("dp", "col"), "row"), P(("dp", "col"), "row"), P("row", "dp", "col"))
    return jax.shard_map(
        on_device, mesh=mesh, in_specs=in_specs, out_specs=out_specs, check_vma=False
    )
```

profile of v0, /device:TPU:0, one launch (start us, length us, event | category | flops | bytes accessed | tf_op | source)
XLA Modules:
  0.0 298.0 jit_solution(7271732196159105316)
XLA Ops:
  7.2 0.0 copy-start.4
  7.2 0.0 copy-start.2
  7.2 0.0 copy-start.3
  7.2 0.0 all-reduce.3.cloned.1.call-start
  7.2 22.5 %copy.8 = bf16[2048,4096]{0,1:T(8,128)(2,1)} copy(bf16[2048,4096]{1,0:T(8,128)(2,1)} %param.6) | data formatting | bytes 33554432 | tf_op args[2]
  29.7 0.0 copy-done.4
  29.7 0.1 copy.7
  29.8 0.1 broadcast_in_dim.6
  29.9 0.0 copy-done.2
  30.0 18.0 %all_gather.6 = bf16[128,2048]{1,0:T(8,128)(2,1)} all-gather(bf16[32,2048]{1,0:T(8,128)(2,1)S(1)} %copy-done.2), channel_id=1, replica_groups=mesh['dp'=2,'row'=4,'col'=4] {'col'}, dimensions={0}, use_global_device_ids=true | all-gather | bytes 655360 | tf_op jit(solution)/shard_map/all_gather | solution.py:41
  48.0 0.0 copy-done.3
  48.0 16.4 %all_gather.7 = bf16[128,2048]{1,0:T(8,128)(2,1)S(1)} all-gather(bf16[32,2048]{1,0:T(8,128)(2,1)S(1)} %copy-done.3), channel_id=1, replica_groups=mesh['dp'=2,'row'=4,'col'=4] {'col'}, dimensions={0}, use_global_device_ids=true | all-gather | bytes 655360 | tf_op jit(solution)/shard_map/all_gather | solution.py:42
  64.3 8.7 %bitcast_multiply_fusion.1 = bf16[2048,4096]{0,1:T(8,128)(2,1)S(1)} fusion(bf16[2048,4096]{0,1:T(8,128)(2,1)} %copy.8, bf16[2048,16]{0,1:T(8,128)(2,1)S(1)} %bitcast.49), kind=kLoop, calls=%fused_computation.3 | loop fusion | flops 8388608 | bytes 33619968 | tf_op jit(solution)/shard_map/mul | solution.py:38
  73.0 0.0 copy-start
  73.0 7.5 %convolution_bitcast_fusion.1 = f32[128,4096]{0,1:T(8,128)} fusion(bf16[2048,4096]{0,1:T(8,128)(2,1)S(1)} %bitcast_multiply_fusion.1, bf16[128,2048]{1,0:T(8,128)(2,1)} %all_gather.6), kind=kOutput, calls=%fused_computation.5 | convolution fusion | flops 2147483648 | bytes 19398656 | tf_op jit(solution)/shard_map/dot_general | solution.py:44
  80.6 0.0 copy-done
  80.6 6.1 %convolution_bitcast_fusion = f32[128,4096]{0,1:T(8,128)} fusion(bf16[2048,4096]{0,1:T(8,128)(2,1)S(1)} %bitcast_multiply_fusion.1, bf16[128,2048]{1,0:T(8,128)(2,1)S(1)} %all_gather.7), kind=kOutput, calls=%fused_computation.4 | convolution fusion | flops 2147483648 | bytes 19398656 | tf_op jit(solution)/shard_map/dot_general | solution.py:47
  86.7 0.0 all-reduce.3.cloned.1.call-update
  86.7 0.2 reduce-scatter.3.cloned.1.call-start
  86.9 104.7 %all-reduce.3.cloned.1.call-done = (f32[128,4096]{0,1:T(8,128)}, f32[128,4096]{0,1:T(8,128)}) async-done(((f32[128,4096]{0,1:T(8,128)}, f32[128,4096]{0,1:T(8,128)}), (f32[128,4096]{0,1:T(8,128)}, f32[128,4096]{0,1:T(8,128)})) %all-reduce.3.cloned.1.call-update) | async-done | bytes 4194320 | tf_op jit(solution)/shard_map/psum | solution.py:45
  191.6 3.2 %multiply_convert_fusion = (bf16[128,4096]{0,1:T(8,128)(2,1)S(1)}, bf16[128,4096]{0,1:T(8,128)(2,1)S(1)}) fusion(f32[128,4096]{0,1:T(8,128)} %get-tuple-element.6, f32[128,4096]{0,1:T(8,128)} %get-tuple-element.7), kind=kLoop, calls=%fused_computation.6 | loop fusion | flops 5767168 | bytes 6291456 | tf_op jit(solution)/shard_map/convert_element_type | solution.py:27
  194.8 9.1 %fusion.15 = f32[128,2048]{1,0:T(8,128)} fusion(bf16[128,4096]{0,1:T(8,128)(2,1)S(1)} %get-tuple-element.9, bf16[2048,4096]{0,1:T(8,128)(2,1)} %copy-done), kind=kOutput, calls=%fused_computation.30 | convolution fusion | flops 2147483648 | bytes 18874368 | tf_op jit(solution)/shard_map/dot_general | solution.py:31
  204.0 0.0 reduce-scatter.3.cloned.1.call-update
  204.0 0.0 reduce-scatter.5.cloned.1.call-start
  204.0 0.1 collective-permute-start.3
  204.1 0.5 collective-permute-start.1
  204.6 1.0 dynamic-slice_bitcast_fusion.1
  205.7 0.1 collective-permute-start.2
  205.7 0.9 dynamic-slice_bitcast_fusion.3
  206.6 0.0 copy-start.1
  206.7 0.4 collective-permute-start
  207.1 9.3 %fusion.16 = f32[128,2048]{1,0:T(8,128)} fusion(bf16[128,4096]{0,1:T(8,128)(2,1)S(1)} %get-tuple-element.8, bf16[2048,4096]{0,1:T(8,128)(2,1)} %copy-done), kind=kOutput, calls=%fused_computation.31 | convolution fusion | flops 2147483648 | bytes 18874368 | tf_op jit(solution)/shard_map/dot_general | solution.py:31
  216.4 0.0 reduce-scatter.5.cloned.1.call-update
  216.4 0.0 collective-permute-done.3
  216.5 0.0 collective-permute-done.2
  216.5 0.0 copy-done.1
  216.5 9.9 %fusion.7 = f32[2048,2048]{1,0:T(8,128)} fusion(bf16[128,1,2048]{0,2,1:T(8,128)(2,1)} %collective-permute-done.2, bf16[128,1,2048]{0,2,1:T(8,128)(2,1)S(1)} %copy-done.1, bf16[128,2048]{1,0:T(8,128)(2,1)} %collective-permute-done.3, bf16[128,2048]{1,0:T(8,128)(2,1)} %all_gather.6), kind=kOutput, calls=%fused_computation.16 | convolution fusion | flops 2151677952 | bytes 18874368 | tf_op jit(solution)/shard_map/td,tqj->qdj/dot_general | solution.py:82
  226.3 0.0 collective-permute-done.1
  226.3 0.0 collective-permute-done
  226.4 6.0 %broadcast_in_dim.7 = bf16[2048,16,256]{0,2,1:T(8,128)(2,1)} broadcast(bf16[2048,16]{0,1:T(8,128)(2,1)S(1)} %bitcast.50), dimensions={0,1} | broadcast | bytes 16842752 | tf_op jit(solution)/shard_map/broadcast_in_dim | solution.py:22
  232.4 16.1 %fusion.1 = f32[2048,1,2048]{0,2,1:T(8,128)} fusion(f32[2048,2048]{1,0:T(8,128)} %fusion.7, bf16[2048,4096]{0,1:T(8,128)(2,1)} %bitcast.46, s32[]{:T(128)S(6)} %select_n.22, bf16[128,1,2048]{0,2,1:T(8,128)(2,1)S(1)} %collective-permute-done, bf16[128,1,2048]{0,2,1:T(8,128)(2,1)S(1)} %get-tuple-element.10, bf16[128,2048]{1,0:T(8,128)(2,1)} %collective-permute-done.1, ...), kind=kOutput, calls=%fused_computation.2 | convolution fusion | flops 2168455168 | bytes 44040196 | tf_op jit(solution)/shard_map/td,tqj->qdj/dot_general | solution.py:79
  248.5 39.8 %copy.9 = f32[2048,1,2048]{2,1,0:T(1,128)} copy(f32[2048,1,2048]{0,2,1:T(8,128)} %fusion.1) | data formatting | bytes 33554432
  288.2 0.0 reduce-scatter.3.cloned.1.call-done
  288.2 1.6 add_convert_fusion.1
  289.8 0.0 reduce-scatter.5.cloned.1.call-done
  289.8 1.6 add_convert_fusion
  (2 shorter events, 0.0 us)
Async XLA Ops:
  7.2 22.6 %copy-start.4 = (s32[8,16]{1,0:T(8,128)S(1)}, s32[8,16]{1,0:T(8,128)}, u32[]{:S(2)}) copy-start(s32[8,16]{1,0:T(8,128)} %param.7) | copy-start | bytes 1540
  7.2 22.8 %copy-start.2 = (bf16[32,2048]{1,0:T(8,128)(2,1)S(1)}, bf16[32,2048]{1,0:T(8,128)(2,1)}, u32[]{:S(2)}) copy-start(bf16[32,2048]{1,0:T(8,128)(2,1)} %param.4) | copy-start | bytes 393220
  7.2 40.8 %copy-start.3 = (bf16[32,2048]{1,0:T(8,128)(2,1)S(1)}, bf16[32,2048]{1,0:T(8,128)(2,1)}, u32[]{:S(2)}) copy-start(bf16[32,2048]{1,0:T(8,128)(2,1)} %param.5) | copy-start | bytes 393220
  7.2 184.4 %all-reduce.3.cloned.1.call-start = ((), (), s32[]{:S(2)}) async-start(), calls=%async_computation.4 | async-start | bytes 8388608 | tf_op jit(solution)/shard_map/psum | solution.py:45
  73.0 7.6 %copy-start = (bf16[2048,4096]{0,1:T(8,128)(2,1)}, bf16[2048,4096]{0,1:T(8,128)(2,1)S(1)}, u32[]{:S(2)}) copy-start(bf16[2048,4096]{0,1:T(8,128)(2,1)S(1)} %bitcast_multiply_fusion.1) | copy-start | bytes 50331652
  86.7 201.5 %reduce-scatter.3.cloned.1.call-start = ((), (), s32[]{:S(2)}) async-start(), calls=%async_computation.2 | async-start | bytes 1310720 | tf_op jit(solution)/shard_map/reduce_scatter | solution.py:50
  204.0 85.8 %reduce-scatter.5.cloned.1.call-start = ((), (), s32[]{:S(2)}) async-start(), calls=%async_computation.3 | async-start | bytes 1310720 | tf_op jit(solution)/shard_map/reduce_scatter | solution.py:54
  204.0 12.4 %collective-permute-start.3 = (bf16[128,2048]{1,0:T(8,128)(2,1)}, bf16[128,2048]{1,0:T(8,128)(2,1)}, u32[]{:S(2)}, u32[]{:S(2)}) collective-permute-start(bf16[128,2048]{1,0:T(8,128)(2,1)} %all_gather.6), channel_id=1, source_target_pairs={{0,16},{16,0},{1,17},{17,1},{2,18},{18,2},{3,19},{19,3},{4,20},{20... | collective-permute-start | bytes 1572872 | tf_op jit(solution)/shard_map/ppermute | solution.py:17
  204.1 22.2 %collective-permute-start.1 = (bf16[128,2048]{1,0:T(8,128)(2,1)S(1)}, bf16[128,2048]{1,0:T(8,128)(2,1)}, u32[]{:S(2)}, u32[]{:S(2)}) collective-permute-start(bf16[128,2048]{1,0:T(8,128)(2,1)S(1)} %all_gather.7), channel_id=1, source_target_pairs={{0,16},{16,0},{1,17},{17,1},{2,18},{18,2},{3,19},{19,3},{4,20},{20... | collective-permute-start | bytes 1572872 | tf_op jit(solution)/shard_map/ppermute | solution.py:17
  205.7 10.8 %collective-permute-start.2 = (bf16[128,1,2048]{0,2,1:T(8,128)(2,1)}, bf16[128,1,2048]{0,2,1:T(8,128)(2,1)}, u32[]{:S(2)}, u32[]{:S(2)}) collective-permute-start(bf16[128,1,2048]{0,2,1:T(8,128)(2,1)} %get-tuple-element.13), channel_id=1, source_target_pairs={{0,16},{16,0},{1,17},{17,1},{2,18},{18,2},{3,19},{19,3},{4,20},{20... | collective-permute-start | bytes 1572872 | tf_op jit(solution)/shard_map/ppermute | solution.py:17
  206.6 9.8 %copy-start.1 = (bf16[128,1,2048]{0,2,1:T(8,128)(2,1)S(1)}, bf16[128,1,2048]{0,2,1:T(8,128)(2,1)}, u32[]{:S(2)}) copy-start(bf16[128,1,2048]{0,2,1:T(8,128)(2,1)} %get-tuple-element.12) | copy-start | bytes 1572868
  206.7 19.7 %collective-permute-start = (bf16[128,1,2048]{0,2,1:T(8,128)(2,1)}, bf16[128,1,2048]{0,2,1:T(8,128)(2,1)S(1)}, u32[]{:S(2)}, u32[]{:S(2)}) collective-permute-start(bf16[128,1,2048]{0,2,1:T(8,128)(2,1)} %get-tuple-element.11), channel_id=1, source_target_pairs={{0,16},{16,0},{1,17},{17,1},{2,18},{18,2},{3,19},{19,3},{4,20},{20... | collective-permute-start | bytes 1572872 | tf_op jit(solution)/shard_map/ppermute | solution.py:17
Sparse Core Ops, SparseCore 0:
  86.8 104.7 all-reduce.2
  204.1 27.2 reduce-scatter.2
  233.7 25.7 reduce-scatter.4
where the time goes:
time: 300 us; the launch traced here: 298 us
  waiting for transfers between devices  105 us (35%)
  local copies, waits for them, and re-layouts  70.4 us (23%)
  matrix products  58.1 us (19%)
  blocking collectives  34.4 us (11%)
  other arithmetic  15.1 us (5%)
  between operations  13.9 us (5%)
    psum x1, waiting for transfers between devices, on_device(): pre = lax.psum(pre_part, 'row')  105 us
    unnamed x13, local copies, waits for them, and re-layouts  62.3 us
    dot_general x2, matrix products, times_transpose(): lax.dot_general(left, masked, (((1,), (1,)), ((), ())), preferred_element...  18.5 us
    all_gather x1, blocking collectives, on_device(): lax.all_gather(tokens, 'col', axis=0, tiled=True)  18 us
    all_gather x1, blocking collectives, on_device(): lax.all_gather(cotangent, 'col', axis=0, tiled=True)  16.4 us
    dot_general x1, matrix products, on_device(): jnp.einsum('td,tqj->qdj', pair_cot, pair_hid, preferred_element_type=jnp....  16.1 us
    dot_general x1, matrix products, on_device(): jnp.einsum('td,tqj->qdj', pair_tok, pair_grad, preferred_element_type=jnp...  9.87 us
    mul x1, other arithmetic, on_device(): masked = weight * kept  8.67 us
  transfers between devices with their start and end apart: 7, of which 1 were waited for; matrix products, arithmetic and copies ran while one was open for 28% of the time, Pallas kernels for 0%

commit v1 on v0

--- a/solution.py
+++ b/solution.py
@@ -5,6 +5,23 @@
 from jax.sharding import PartitionSpec as P
 
 BLOCK = 256
+
+
+def joined_along(blocks, dim):
+    blocks = jnp.moveaxis(blocks, 0, dim)
+    shape = blocks.shape
+    return blocks.reshape(*shape[:dim], shape[dim] * shape[dim + 1], *shape[dim + 2 :])
+
+
+def collect(array, axis, dim):
+    devices = lax.axis_size(axis)
+    right = [(i, (i + 1) % devices) for i in range(devices)]
+    tiles = [array]
+    while len(tiles) < devices:
+        tiles.append(lax.ppermute(tiles[-1], axis, right))
+    mine = lax.axis_index(axis)
+    tiles = jnp.stack(tiles)[(mine - jnp.arange(devices)) % devices]
+    return joined_along(tiles, dim)
 
 
 def partner(block, axis, stride):
@@ -38,7 +55,7 @@
     masked = weight * kept
     tok_count = tokens.shape[0]
     tok_rows, cot_rows = (
-        lax.all_gather(tokens, "col", axis=0, tiled=True),
+        collect(tokens, "col", 0),
         lax.all_gather(cotangent, "col", axis=0, tiled=True),
     )
     pre_part = jnp.dot(tok_rows, masked, preferred_element_type=jnp.float32)

time: 300 us -> 306 us (1.020)
  blocking collectives: 34.4 us -> 15.8 us
  local copies, waits for them, and re-layouts: 70.4 us -> 79.4 us
  matrix products: 58.1 us -> 65.3 us
  starting transfers between devices: 1.38 us -> 5.76 us
  waiting for transfers between devices: 105 us -> 109 us
    all_gather x1 -> x0, blocking collectives: 18 us -> none  [on_device(): lax.all_gather(tokens, 'col', axis=0, tiled=True)]
    ppermute x0 -> x3, waiting for transfers between devices: none -> 6.44 us  [collect(): tiles.append(lax.ppermute(tiles[-1], axis, right))]
    dot_general x1, matrix products: 7.54 us -> 12.9 us  [on_device(): pre_part = jnp.dot(tok_rows, masked, preferred_element_type=jnp.float32)]
    ppermute x0 -> x3, starting transfers between devices: none -> 4.41 us  [collect(): tiles.append(lax.ppermute(tiles[-1], axis, right))]
    dynamic_slice x0 -> x2, local copies, waits for them, and re-layouts: none -> 4.33 us  [the longest x1 2.17 us: on_device(): lax.dynamic_index_in_dim(grad_split, low_bit, 2, keepdims=False)]
    unnamed x13 -> x17, local copies, waits for them, and re-layouts: 62.3 us -> 65.9 us
  transfers between devices with their start and end apart: 7 -> 10, of which waited for: 1 -> 2; matrix products, arithmetic and copies ran while one was open for 28% -> 43% of each run, Pallas kernels for 0% -> 0%
where the time goes in v1:
time: 306 us; the launch traced here: 304 us
  waiting for transfers between devices  109 us (36%)
  local copies, waits for them, and re-layouts  79.4 us (26%)
  matrix products  65.3 us (21%)
  blocking collectives  15.8 us (5%)
  other arithmetic  15.2 us (5%)
  between operations  13.9 us (5%)
  starting transfers between devices  5.76 us (2%)
    psum x1, waiting for transfers between devices, on_device(): pre = lax.psum(pre_part, 'row')  102 us
    unnamed x17, local copies, waits for them, and re-layouts  65.9 us
    dot_general x2, matrix products, times_transpose(): lax.dot_general(left, masked, (((1,), (1,)), ((), ())), preferred_element...  18.3 us
    dot_general x1, matrix products, on_device(): jnp.einsum('td,tqj->qdj', pair_cot, pair_hid, preferred_element_type=jnp....  16.1 us
    all_gather x1, blocking collectives, on_device(): lax.all_gather(cotangent, 'col', axis=0, tiled=True)  15.8 us
    dot_general x1, matrix products, on_device(): pre_part = jnp.dot(tok_rows, masked, preferred_element_type=jnp.float32)  12.9 us
    dot_general x1, matrix products, on_device(): jnp.einsum('td,tqj->qdj', pair_tok, pair_grad, preferred_element_type=jnp...  9.92 us
    mul x1, other arithmetic, on_device(): masked = weight * kept  8.71 us
  transfers between devices with their start and end apart: 10, of which 2 were waited for; matrix products, arithmetic and copies ran while one was open for 43% of the time, Pallas kernels for 0%

profile of v1, /device:TPU:0, one launch (start us, length us, event | category | flops | bytes accessed | tf_op | source)
XLA Modules:
  0.0 304.0 jit_solution(4438465866569541701)
XLA Ops:
  7.2 0.0 all-reduce.3.cloned.1.call-start
  7.2 3.1 %collective-permute-start = (bf16[32,2048]{1,0:T(8,128)(2,1)}, bf16[32,2048]{1,0:T(8,128)(2,1)S(1)}, u32[]{:S(2)}, u32[]{:S(2)}) collective-permute-start(bf16[32,2048]{1,0:T(8,128)(2,1)} %param.4), channel_id=1, source_target_pairs={{0,1},{1,2},{2,3},{3,0},{4,5},{5,6},{6,7},{7,4},{8,9},{9,10},{10,1... | collective-permute-start | bytes 393224 | tf_op jit(solution)/shard_map/ppermute | solution.py:21
  10.3 22.4 %copy.12 = bf16[2048,4096]{0,1:T(8,128)(2,1)} copy(bf16[2048,4096]{1,0:T(8,128)(2,1)} %param.6) | data formatting | bytes 33554432 | tf_op args[2]
  32.8 0.1 copy.11
  32.9 0.1 broadcast_in_dim.7
  33.0 0.0 copy-start.2
  33.0 8.7 %bitcast_multiply_fusion.1 = bf16[2048,4096]{0,1:T(8,128)(2,1)S(1)} fusion(bf16[2048,4096]{0,1:T(8,128)(2,1)} %copy.12, bf16[2048,16]{0,1:T(8,128)(2,1)S(1)} %bitcast.56), kind=kLoop, calls=%fused_computation.4 | loop fusion | flops 8388608 | bytes 33619968 | tf_op jit(solution)/shard_map/mul | solution.py:55
  41.7 0.0 copy-start
  41.7 15.8 %all_gather.3 = bf16[128,2048]{1,0:T(8,128)(2,1)} all-gather(bf16[32,2048]{1,0:T(8,128)(2,1)S(1)} %copy-done.2), channel_id=1, replica_groups=mesh['dp'=2,'row'=4,'col'=4] {'col'}, dimensions={0}, use_global_device_ids=true | all-gather | bytes 655360 | tf_op jit(solution)/shard_map/all_gather | solution.py:59
  57.5 0.0 collective-permute-done
  57.5 1.0 collective-permute-start.1
  58.5 8.0 %convolution_bitcast_fusion = f32[128,4096]{1,0:T(8,128)} fusion(bf16[2048,4096]{0,1:T(8,128)(2,1)S(1)} %bitcast_multiply_fusion.1, bf16[128,2048]{1,0:T(8,128)(2,1)} %all_gather.3), kind=kOutput, calls=%fused_computation.5 | convolution fusion | flops 2147483648 | bytes 19398656 | tf_op jit(solution)/shard_map/dot_general | solution.py:64
  66.5 0.0 collective-permute-done.1
  66.5 0.3 collective-permute-start.2
  66.8 6.4 %collective-permute-done.2 = bf16[32,2048]{1,0:T(8,128)(2,1)S(1)} collective-permute-done((bf16[32,2048]{1,0:T(8,128)(2,1)S(1)}, bf16[32,2048]{1,0:T(8,128)(2,1)S(1)}, u32[]{:S(2)}, u32[]{:S(2)}) %collective-permute-start.2) | collective-permute-done | bytes 131104 | tf_op jit(solution)/shard_map/ppermute | solution.py:21
  73.3 0.1 pad_maximum_fusion
  73.3 1.4 gather_fusion
  74.8 12.9 %fusion.17 = f32[128,4096]{1,0:T(8,128)} fusion(bf16[128,2048]{1,0:T(8,128)(2,1)} %bitcast.5, bf16[2048,4096]{0,1:T(8,128)(2,1)} %copy-done), kind=kOutput, calls=%fused_computation.42 | convolution fusion | flops 2147483648 | bytes 19398656 | tf_op jit(solution)/shard_map/dot_general | solution.py:61
  87.7 0.0 all-reduce.3.cloned.1.call-update
  87.7 0.2 reduce-scatter.3.cloned.1.call-start
  87.9 102.3 %all-reduce.3.cloned.1.call-done = (f32[128,4096]{1,0:T(8,128)}, f32[128,4096]{1,0:T(8,128)}) async-done(((f32[128,4096]{1,0:T(8,128)}, f32[128,4096]{1,0:T(8,128)}), (f32[128,4096]{1,0:T(8,128)}, f32[128,4096]{1,0:T(8,128)})) %all-reduce.3.cloned.1.call-update) | async-done | bytes 4194320 | tf_op jit(solution)/shard_map/psum | solution.py:62
  190.2 3.1 %multiply_convert_fusion = (bf16[128,4096]{1,0:T(8,128)(2,1)S(1)}, bf16[128,4096]{1,0:T(8,128)(2,1)S(1)}) fusion(f32[128,4096]{1,0:T(8,128)} %get-tuple-element.9, f32[128,4096]{1,0:T(8,128)} %get-tuple-element.10), kind=kLoop, calls=%fused_computation.6 | loop fusion | flops 5767168 | bytes 6291456 | tf_op jit(solution)/shard_map/convert_element_type | solution.py:44
  193.3 9.1 %fusion.18 = f32[128,2048]{1,0:T(8,128)} fusion(bf16[128,4096]{1,0:T(8,128)(2,1)S(1)} %get-tuple-element.12, bf16[2048,4096]{0,1:T(8,128)(2,1)} %copy-done), kind=kOutput, calls=%fused_computation.43 | convolution fusion | flops 2147483648 | bytes 18874368 | tf_op jit(solution)/shard_map/dot_general | solution.py:48
  202.4 0.0 reduce-scatter.3.cloned.1.call-update
  202.4 0.0 reduce-scatter.5.cloned.1.call-start
  202.5 0.1 collective-permute-start.4
  202.6 0.5 collective-permute-start.6
  203.0 0.8 reshape.85
  203.8 0.8 reshape.87
  204.6 2.2 constant_dynamic-slice_fusion.1
  206.8 1.1 copy.29
  207.9 0.1 collective-permute-start.5
  208.0 1.1 copy.30
  209.2 2.2 constant_dynamic-slice_fusion.3
  211.3 1.1 copy.31
  212.4 0.4 collective-permute-start.3
  212.9 0.3 copy.32
  213.2 9.2 %fusion.19 = f32[128,2048]{1,0:T(8,128)} fusion(bf16[128,4096]{1,0:T(8,128)(2,1)S(1)} %get-tuple-element.11, bf16[2048,4096]{0,1:T(8,128)(2,1)} %copy-done), kind=kOutput, calls=%fused_computation.44 | convolution fusion | flops 2147483648 | bytes 18874368 | tf_op jit(solution)/shard_map/dot_general | solution.py:48
  222.4 0.0 reduce-scatter.5.cloned.1.call-update
  222.4 0.0 collective-permute-done.6
  222.4 0.0 collective-permute-done.5
  222.4 9.9 %fusion.7 = f32[2048,2048]{1,0:T(8,128)} fusion(bf16[128,1,2048]{2,0,1:T(8,128)(2,1)} %collective-permute-done.5, bf16[128,1,2048]{2,0,1:T(8,128)(2,1)S(1)} %bitcast.55, bf16[128,2048]{1,0:T(8,128)(2,1)} %collective-permute-done.6, bf16[128,2048]{1,0:T(8,128)(2,1)} %bitcast.5), kind=kOutput, calls=%fused_computation.16 | convolution fusion | flops 2151677952 | bytes 18874368 | tf_op jit(solution)/shard_map/td,tqj->qdj/dot_general | solution.py:99
  232.4 0.0 collective-permute-done.4
  232.4 6.0 %broadcast_in_dim.8 = bf16[2048,16,256]{0,2,1:T(8,128)(2,1)} broadcast(bf16[2048,16]{0,1:T(8,128)(2,1)S(1)} %bitcast.57), dimensions={0,1} | broadcast | bytes 16842752 | tf_op jit(solution)/shard_map/broadcast_in_dim | solution.py:39
  238.4 16.1 %fusion.1 = f32[2048,1,2048]{0,2,1:T(8,128)} fusion(f32[2048,2048]{1,0:T(8,128)} %fusion.7, bf16[2048,4096]{0,1:T(8,128)(2,1)} %bitcast.53, s32[]{:T(128)S(6)} %select_n.47, bf16[128,1,2048]{2,0,1:T(8,128)(2,1)S(1)} %collective-permute-done.3, bf16[128,1,2048]{2,0,1:T(8,128)(2,1)S(1)} %bitcast.54, bf16[128,2048]{1,0:T(8,128)(2,1)} %collective-permute-done.4, ...), kind=kOutput, calls=%fused_computation.3 | convolution fusion | flops 2168455168 | bytes 44040196 | tf_op jit(solution)/shard_map/td,tqj->qdj/dot_general | solution.py:96
  254.5 39.7 %copy.18 = f32[2048,1,2048]{2,1,0:T(1,128)} copy(f32[2048,1,2048]{0,2,1:T(8,128)} %fusion.1) | data formatting | bytes 33554432
  294.2 1.6 add_convert_fusion.1
  295.9 1.6 add_convert_fusion
  (15 shorter events, 0.1 us)
Async XLA Ops:
  7.2 25.6 %copy-start.4 = (s32[8,16]{1,0:T(8,128)S(1)}, s32[8,16]{1,0:T(8,128)}, u32[]{:S(2)}) copy-start(s32[8,16]{1,0:T(8,128)} %param.7) | copy-start | bytes 1540
  7.2 183.0 %all-reduce.3.cloned.1.call-start = ((), (), s32[]{:S(2)}) async-start(), calls=%async_computation.4 | async-start | bytes 8388608 | tf_op jit(solution)/shard_map/psum | solution.py:62
  7.2 50.3 %collective-permute-start = (bf16[32,2048]{1,0:T(8,128)(2,1)}, bf16[32,2048]{1,0:T(8,128)(2,1)S(1)}, u32[]{:S(2)}, u32[]{:S(2)}) collective-permute-start(bf16[32,2048]{1,0:T(8,128)(2,1)} %param.4), channel_id=1, source_target_pairs={{0,1},{1,2},{2,3},{3,0},{4,5},{5,6},{6,7},{7,4},{8,9},{9,10},{10,1... | collective-permute-start | bytes 393224 | tf_op jit(solution)/shard_map/ppermute | solution.py:21
  33.0 8.7 %copy-start.2 = (bf16[32,2048]{1,0:T(8,128)(2,1)S(1)}, bf16[32,2048]{1,0:T(8,128)(2,1)}, u32[]{:S(2)}) copy-start(bf16[32,2048]{1,0:T(8,128)(2,1)} %param.5) | copy-start | bytes 393220
  41.7 24.8 %copy-start = (bf16[2048,4096]{0,1:T(8,128)(2,1)}, bf16[2048,4096]{0,1:T(8,128)(2,1)S(1)}, u32[]{:S(2)}) copy-start(bf16[2048,4096]{0,1:T(8,128)(2,1)S(1)} %bitcast_multiply_fusion.1) | copy-start | bytes 50331652
  57.5 15.8 %copy-start.3 = (bf16[32,2048]{1,0:T(8,128)(2,1)S(1)}, bf16[32,2048]{1,0:T(8,128)(2,1)}, u32[]{:S(2)}) copy-start(bf16[32,2048]{1,0:T(8,128)(2,1)} %param.4) | copy-start | bytes 393220
  57.5 9.0 %collective-permute-start.1 = (bf16[32,2048]{1,0:T(8,128)(2,1)S(1)}, bf16[32,2048]{1,0:T(8,128)(2,1)S(1)}, u32[]{:S(2)}, u32[]{:S(2)}) collective-permute-start(bf16[32,2048]{1,0:T(8,128)(2,1)S(1)} %collective-permute-done), channel_id=1, source_target_pairs={{0,1},{1,2},{2,3},{3,0},{4,5},{5,6},{6,7},{7,4},{8,9},{9,10},{10,1... | collective-permute-start | bytes 393224 | tf_op jit(solution)/shard_map/ppermute | solution.py:21
  66.5 6.8 %collective-permute-start.2 = (bf16[32,2048]{1,0:T(8,128)(2,1)S(1)}, bf16[32,2048]{1,0:T(8,128)(2,1)S(1)}, u32[]{:S(2)}, u32[]{:S(2)}) collective-permute-start(bf16[32,2048]{1,0:T(8,128)(2,1)S(1)} %collective-permute-done.1), channel_id=1, source_target_pairs={{0,1},{1,2},{2,3},{3,0},{4,5},{5,6},{6,7},{7,4},{8,9},{9,10},{10,1... | collective-permute-start | bytes 393224 | tf_op jit(solution)/shard_map/ppermute | solution.py:21
  87.7 206.5 %reduce-scatter.3.cloned.1.call-start = ((), (), s32[]{:S(2)}) async-start(), calls=%async_computation.2 | async-start | bytes 1310720 | tf_op jit(solution)/shard_map/reduce_scatter | solution.py:67
  202.4 93.5 %reduce-scatter.5.cloned.1.call-start = ((), (), s32[]{:S(2)}) async-start(), calls=%async_computation.3 | async-start | bytes 1310720 | tf_op jit(solution)/shard_map/reduce_scatter | solution.py:71
  202.5 29.9 %collective-permute-start.4 = (bf16[128,2048]{1,0:T(8,128)(2,1)}, bf16[128,2048]{1,0:T(8,128)(2,1)}, u32[]{:S(2)}, u32[]{:S(2)}) collective-permute-start(bf16[128,2048]{1,0:T(8,128)(2,1)} %all_gather.3), channel_id=1, source_target_pairs={{0,16},{16,0},{1,17},{17,1},{2,18},{18,2},{3,19},{19,3},{4,20},{20... | collective-permute-start | bytes 1572872 | tf_op jit(solution)/shard_map/ppermute | solution.py:34
  202.6 19.8 %collective-permute-start.6 = (bf16[128,2048]{1,0:T(8,128)(2,1)}, bf16[128,2048]{1,0:T(8,128)(2,1)}, u32[]{:S(2)}, u32[]{:S(2)}) collective-permute-start(bf16[128,2048]{1,0:T(8,128)(2,1)} %bitcast.5), channel_id=1, source_target_pairs={{0,16},{16,0},{1,17},{17,1},{2,18},{18,2},{3,19},{19,3},{4,20},{20... | collective-permute-start | bytes 1572872 | tf_op jit(solution)/shard_map/ppermute | solution.py:34
  207.9 14.5 %collective-permute-start.5 = (bf16[128,1,2048]{2,0,1:T(8,128)(2,1)}, bf16[128,1,2048]{2,0,1:T(8,128)(2,1)}, u32[]{:S(2)}, u32[]{:S(2)}) collective-permute-start(bf16[128,1,2048]{2,0,1:T(8,128)(2,1)} %bitcast.49), channel_id=1, source_target_pairs={{0,16},{16,0},{1,17},{17,1},{2,18},{18,2},{3,19},{19,3},{4,20},{20... | collective-permute-start | bytes 1572872 | tf_op jit(solution)/shard_map/ppermute | solution.py:34
  212.4 19.9 %collective-permute-start.3 = (bf16[128,1,2048]{2,0,1:T(8,128)(2,1)}, bf16[128,1,2048]{2,0,1:T(8,128)(2,1)S(1)}, u32[]{:S(2)}, u32[]{:S(2)}) collective-permute-start(bf16[128,1,2048]{2,0,1:T(8,128)(2,1)} %bitcast.51), channel_id=1, source_target_pairs={{0,16},{16,0},{1,17},{17,1},{2,18},{18,2},{3,19},{19,3},{4,20},{20... | collective-permute-start | bytes 1572872 | tf_op jit(solution)/shard_map/ppermute | solution.py:34
  213.2 9.3 %copy-start.1 = (bf16[128,1,1,2048]{3,0,2,1:T(8,128)(2,1)S(1)}, bf16[128,1,1,2048]{3,0,2,1:T(8,128)(2,1)}, u32[]{:S(2)}) copy-start(bf16[128,1,1,2048]{3,0,2,1:T(8,128)(2,1)} %copy.30) | copy-start | bytes 1572868
Sparse Core Ops, SparseCore 0:
  87.8 102.3 all-reduce.2
  202.5 27.2 reduce-scatter.2
  232.2 25.7 reduce-scatter.4
